TPU v7x, 32 devices: a whole 2x2x4 slice. The times are simulated.
32 devices in a mesh: frame: 4 (over y, x), sector: 8 (over z, core).
Axes of the slice: x: 2, y: 2, z: 4, core: 2. Of those that a mesh axis runs over, the one named last changes fastest.
Arguments:
- camera: bfloat16 [4096, 1536], P(('frame', 'sector')), may hold values from -6 to 6
- owners: int32 [256], P(('frame', 'sector')), may hold values from 0 to 7, as said below
- unit_slots: int32 [256, 8], P(('frame', 'sector')), may hold values from 0 to 15, as said below
- pool_weights: bfloat16 [256, 8, 16, 128], P(('frame', 'sector')), may hold values from -0.0234375 to 0.0234375
- student: bfloat16 [32768, 512], P(('frame', 'sector')), may hold values from -0.25 to 0.25
- head_weight: bfloat16 [1536, 512], replicated, may hold values from -0.15625 to 0.15625
Outputs:
- grad_student: bfloat16 [32768, 512], P(('frame', 'sector'))
- grad_head: float32 [1536, 512], P('sector')
Inputs may be any that keep to these rules, and one draw needn't show every extreme that they name: `owners`: in every frame group a device sends at most 2 of its units to any one sector, one sector receives exactly 2 units from every device of the group, and every sector receives at least one unit. `unit_slots`: an entry q of a lidar block held by sector o of frame group f names the unit of rank q % 2 among the units of device q // 2 of group f that are owned by o; that unit exists, and every unit is named by at least one entry of its owner.
All inputs are finite; a program needn't handle non-finite values.
Results may differ from a plain program's by a relative error of at most 0.005.
Values may be sent and summed in bfloat16 or wider, within the bound.
A program may use at most 64 MiB of HBM per device.

v0:
```python
import jax
import jax.numpy as jnp
from jax import lax
from jax.sharding import PartitionSpec as P

CAP = 2
LOSS_WEIGHT = 8.0
EPSILON = 1e-06


def cosine_grads(target, student):
    learner = student.astype(jnp.float32)
    norm_teacher = jnp.sqrt(jnp.sum(target * target, axis=-1, keepdims=True) + EPSILON)
    norm_learner = jnp.sqrt(jnp.sum(learner * learner, axis=-1, keepdims=True) + EPSILON)
    cosine = jnp.sum(target * learner, axis=-1, keepdims=True) / (norm_teacher * norm_learner)
    grad_learner = -LOSS_WEIGHT * (
        target / (norm_teacher * norm_learner) - cosine * learner / (norm_learner * norm_learner)
    )
    grad_teacher = -LOSS_WEIGHT * (
        learner / (norm_teacher * norm_learner) - cosine * target / (norm_teacher * norm_teacher)
    )
    return (grad_teacher.astype(jnp.bfloat16), grad_learner.astype(jnp.bfloat16))


def project_rows(features, head_weight):
    return jnp.dot(features, head_weight, preferred_element_type=jnp.float32).astype(jnp.bfloat16)


def on_device(camera, owners, unit_slots, pool_weights, student, head_weight):
    sectors = lax.axis_size("sector")
    count_units = owners.shape[0]
    unit_rows = camera.shape[0] // count_units
    width = camera.shape[1]
    head_width = head_weight.shape[1]
    blocks, per_block = unit_slots.shape
    block_rows = pool_weights.shape[3]
    earlier = jnp.arange(count_units)[:, None] > jnp.arange(count_units)[None, :]
    matching = owners[:, None] == owners[None, :]
    rank_of = jnp.sum(jnp.where(earlier & matching, 1, 0), axis=1).astype(jnp.int32)
    destination = owners * CAP + rank_of
    placing = (jnp.arange(sectors * CAP)[:, None] == destination[None, :]).astype(jnp.bfloat16)
    flat_slots = unit_slots.reshape(-1)
    packed = jnp.dot(
        placing, camera.reshape(count_units, unit_rows * width), preferred_element_type=jnp.float32
    ).astype(jnp.bfloat16)
    packed = packed.reshape(sectors, CAP, unit_rows, width)
    arrived = lax.all_to_all(packed, "sector", split_axis=0, concat_axis=0, tiled=True).reshape(
        sectors * CAP * unit_rows, width
    )
    slot_proj = project_rows(arrived, head_weight).reshape(sectors * CAP, unit_rows, head_width)
    chosen = jnp.take(slot_proj, flat_slots, axis=0).reshape(
        blocks, per_block, unit_rows, head_width
    )
    target = jnp.einsum(
        "bkjl,bkjh->blh", pool_weights, chosen, preferred_element_type=jnp.float32
    ).reshape(blocks * block_rows, head_width)
    grad_teacher, grad_student = cosine_grads(target, student)
    spread = jnp.einsum(
        "bkjl,blh->bkjh",
        pool_weights,
        grad_teacher.reshape(blocks, block_rows, head_width),
        preferred_element_type=jnp.float32,
    )
    slot_grad = jax.ops.segment_sum(
        spread.reshape(blocks * per_block, unit_rows * head_width),
        flat_slots,
        num_segments=sectors * CAP,
    ).astype(jnp.bfloat16)
    row_grads = slot_grad.reshape(sectors * CAP * unit_rows, head_width)
    sector_sums = lax.psum_scatter(
        lax.dot_general(
            arrived, row_grads, (((0,), (0,)), ((), ())), preferred_element_type=jnp.float32
        ),
        "sector",
        scatter_dimension=0,
        tiled=True,
    )
    grad_head = lax.psum(sector_sums, "frame")
    return (grad_student, grad_head)


def solution(mesh):
    return jax.shard_map(
        on_device,
        mesh=mesh,
        in_specs=(
            P(("frame", "sector"), None),
            P(("frame", "sector")),
            P(("frame", "sector"), None),
            P(("frame", "sector"), None, None, None),
            P(("frame", "sector"), None),
            P(),
        ),
        out_specs=(P(("frame", "sector"), None), P("sector", None)),
        check_vma=False,
    )
```

profile of v0, /device:TPU:0, one launch (start us, length us, event | category | flops | bytes accessed | tf_op | source)
XLA Modules:
  0.0 148.0 jit_solution(6833077229085780709)
XLA Ops:
  7.2 0.0 copy-start
  7.2 1.3 reshape.112
  8.5 0.9 select_reduce_fusion
  9.4 0.7 multiply_add_fusion
  10.1 0.3 convolution_convert_fusion
  10.4 1.1 copy.10
  11.5 6.3 %all-to-all-start = ((bf16[8,2,16,1536]{3,2,1,0:T(8,128)(2,1)}), bf16[8,2,16,1536]{3,2,1,0:T(8,128)(2,1)S(1)}, u32[]{:S(2)}, u32[]{:S(2)}) async-start(bf16[8,2,16,1536]{3,2,1,0:T(8,128)(2,1)} %bitcast.19), calls=%async_computation | async-start | bytes 1572864 | tf_op jit(solution)/shard_map/all_to_all | solution.py:47
  17.9 0.0 reduce-scatter.2.cloned.1.call-start
  17.9 0.0 copy-done.5
  17.9 0.1 reshape.116
  18.0 0.1 reshape.131
  18.1 20.7 %all-to-all-done = bf16[8,2,16,1536]{3,2,1,0:T(8,128)(2,1)S(1)} async-done(((bf16[8,2,16,1536]{3,2,1,0:T(8,128)(2,1)}), bf16[8,2,16,1536]{3,2,1,0:T(8,128)(2,1)S(1)}, u32[]{:S(2)}, u32[]{:S(2)}) %all-to-all-start) | async-done | bytes 786464 | tf_op jit(solution)/shard_map/all_to_all | solution.py:47
  38.8 0.0 copy-done
  38.8 0.6 convolution_convert_fusion.1
  39.4 0.3 copy-done.2
  39.7 0.6 gather_fusion
  40.4 0.0 copy-start.1
  40.4 0.6 fusion.9
  41.0 0.6 copy-done.1
  41.6 0.4 fusion.1
  42.0 2.2 %fusion.7 = (bf16[1024,512]{1,0:T(8,128)(2,1)S(1)}, bf16[1024,512]{1,0:T(8,128)(2,1)}) fusion(bf16[1024,512]{1,0:T(8,128)(2,1)S(1)} %copy-done.1, f32[8,512,128,1]{1,2,3,0:T(8,128)S(1)} %get-tuple-element.11, f32[1024]{0:T(1024)S(1)} %get-tuple-element.8, f32[1024]{0:T(1024)S(1)} %get-tuple-element.4, f32[1024]{0:T(1024)S(1)} %get-tuple-element.5, ...), kind=kLoop, calls=%fused_computation.14 | loop fusion | flops 6815744 | bytes 5259264 | tf_op jit(solution)/shard_map/convert_element_type | solution.py:22
  44.2 0.4 convolution_bitcast_fusion
  44.6 2.5 %copy.11 = f32[8,8,16,512]{3,1,2,0:T(8,128)} copy(f32[8,8,16,512]{3,2,1,0:T(8,128)S(1)} %convolution_bitcast_fusion) | data formatting | bytes 4194304
  47.2 4.2 %scatter_custom_fusion = f32[16,8192]{1,0:T(8,128)S(1)} fusion(s32[64]{0:T(128)S(1)} %reshape.131, f32[64,8192]{1,0:T(8,128)} %bitcast.55, f32[]{:T(128)} %constant.8.clone.1), kind=kCustom, calls=%fused_computation.27 | custom fusion | flops 524288 | bytes 524800 | tf_op jit(solution)/shard_map/scatter-add | solution.py:64
  51.4 0.1 reshape.120
  51.5 2.3 %fusion.23 = f32[1536,512]{1,0:T(8,128)} fusion(bf16[256,1536]{1,0:T(8,128)(2,1)S(1)} %bitcast.53, bf16[256,512]{1,0:T(8,128)(2,1)S(1)} %reshape.120), kind=kOutput, calls=%fused_computation.47 | convolution fusion | flops 402653184 | bytes 4194304 | tf_op jit(solution)/shard_map/dot_general | solution.py:71
  53.8 0.0 reduce-scatter.2.cloned.1.call-update
  53.8 0.0 all-reduce.2.cloned.1.call-start
  53.9 39.4 %reduce-scatter.2.cloned.1.call-done = f32[192,512]{1,0:T(8,128)} async-done(((f32[1536,512]{1,0:T(8,128)}), f32[192,512]{1,0:T(8,128)}) %reduce-scatter.2.cloned.1.call-update) | async-done | bytes 393232 | tf_op jit(solution)/shard_map/reduce_scatter | solution.py:70
  93.2 0.0 all-reduce.2.cloned.1.call-update
  93.2 46.1 %all-reduce.2.cloned.1.call-done = f32[192,512]{1,0:T(8,128)} async-done(((f32[192,512]{1,0:T(8,128)}), f32[192,512]{1,0:T(8,128)}) %all-reduce.2.cloned.1.call-update) | async-done | bytes 393232 | tf_op jit(solution)/shard_map/psum | solution.py:78
  139.4 1.8 %copy.13 = f32[192,512]{1,0:T(8,128)} copy(f32[192,512]{1,0:T(8,128)} %all-reduce.2.cloned.1.call-done) | data formatting | bytes 786432
  (11 shorter events, 0.1 us)
Async XLA Ops:
  7.2 31.7 %copy-start = (bf16[1536,512]{1,0:T(8,128)(2,1)S(1)}, bf16[1536,512]{1,0:T(8,128)(2,1)}, u32[]{:S(2)}) copy-start(bf16[1536,512]{1,0:T(8,128)(2,1)} %param.11) | copy-start | bytes 4718596
  10.1 7.8 %copy-start.5 = (s32[8,8]{1,0:T(8,128)S(1)}, s32[8,8]{1,0:T(8,128)}, u32[]{:S(2)}) copy-start(s32[8,8]{1,0:T(8,128)} %param.8) | copy-start | bytes 772
  11.5 27.3 %all-to-all-start = ((bf16[8,2,16,1536]{3,2,1,0:T(8,128)(2,1)}), bf16[8,2,16,1536]{3,2,1,0:T(8,128)(2,1)S(1)}, u32[]{:S(2)}, u32[]{:S(2)}) async-start(bf16[8,2,16,1536]{3,2,1,0:T(8,128)(2,1)} %bitcast.19), calls=%async_computation | async-start | bytes 1572864 | tf_op jit(solution)/shard_map/all_to_all | solution.py:47
  17.9 75.4 %reduce-scatter.2.cloned.1.call-start = ((), (), s32[]{:S(2)}) async-start(), calls=%async_computation.2 | async-start | bytes 3538944 | tf_op jit(solution)/shard_map/reduce_scatter | solution.py:70
  38.8 0.9 copy-start.2
  38.8 1.5 %copy-start.4 = (bf16[8,8,16,128]{3,2,1,0:T(8,128)(2,1)S(1)}, bf16[8,8,16,128]{3,2,1,0:T(8,128)(2,1)}, u32[]{:S(2)}) copy-start(bf16[8,8,16,128]{3,2,1,0:T(8,128)(2,1)} %param.9) | copy-start | bytes 786436
  40.4 1.2 copy-start.1
  44.6 6.9 %copy-start.3 = (bf16[8,2,16,1536]{3,2,1,0:T(8,128)(2,1)S(1)}, bf16[8,2,16,1536]{3,2,1,0:T(8,128)(2,1)}, u32[]{:S(2)}) copy-start(bf16[8,2,16,1536]{3,2,1,0:T(8,128)(2,1)} %copy-done.2) | copy-start | bytes 2359300
  53.8 85.6 %all-reduce.2.cloned.1.call-start = ((), (), s32[]{:S(2)}) async-start(), calls=%async_computation.3 | async-start | bytes 786432 | tf_op jit(solution)/shard_map/psum | solution.py:78
Sparse Core Ops, SparseCore 0:
  53.9 39.2 reduce-scatter.1
  96.2 43.1 all-reduce.1
where the time goes:
time: 148 us
  waiting for transfers between devices  106 us (72%)
  between operations  14.2 us (10%)
  local copies, waits for them, and re-layouts  8.6 us (6%)
  other arithmetic  8.37 us (6%)
  starting transfers between devices  6.41 us (4%)
  matrix products  4.19 us (3%)
    psum x1, waiting for transfers between devices, on_device(): grad_head = lax.psum(sector_sums, 'frame')  46.1 us
    reduce_scatter x1, waiting for transfers between devices, on_device(): lax.psum_scatter(lax.dot_general(arrived, row_grads, (((0,), (0,)), ((),...  39.4 us
    all_to_all x1, waiting for transfers between devices, on_device(): lax.all_to_all(packed, 'sector', split_axis=0, concat_axis=0, tiled=True)  20.7 us
    unnamed x15, local copies, waits for them, and re-layouts  6.41 us
    all_to_all x1, starting transfers between devices, on_device(): lax.all_to_all(packed, 'sector', split_axis=0, concat_axis=0, tiled=True)  6.33 us
    scatter-add x1, other arithmetic, on_device(): jax.ops.segment_sum(spread.reshape(blocks * per_block, unit_rows * head_w...  4.17 us
  transfers between devices with their start and end apart: 3, of which 3 were waited for; matrix products, arithmetic and copies ran while one was open for 0% of the time, Pallas kernels for 0%

commit v1 on v0

--- a/solution.py
+++ b/solution.py
@@ -75,7 +75,7 @@
         scatter_dimension=0,
         tiled=True,
     )
-    grad_head = lax.psum(sector_sums, "frame")
+    grad_head = jnp.sum(lax.all_gather(sector_sums, "frame"), axis=0)
     return (grad_student, grad_head)
 
 

time: 148 us -> 135 us (0.912)
  waiting for transfers between devices: 106 us -> 92 us
  other arithmetic: 8.37 us -> 10.7 us
  local copies, waits for them, and re-layouts: 8.6 us -> 6.83 us
    psum x1 -> x0, waiting for transfers between devices: 46.1 us -> none  [on_device(): grad_head = lax.psum(sector_sums, 'frame')]
    all_gather x0 -> x1, waiting for transfers between devices: none -> 31.9 us  [on_device(): grad_head = jnp.sum(lax.all_gather(sector_sums, 'frame'), axis=0)]
    reduce_sum x0 -> x1, other arithmetic: none -> 2.34 us  [on_device(): grad_head = jnp.sum(lax.all_gather(sector_sums, 'frame'), axis=0)]
    unnamed x15 -> x14, local copies, waits for them, and re-layouts: 6.41 us -> 4.64 us
where the time goes in v1:
time: 135 us; the launch traced here: 134 us
  waiting for transfers between devices  92 us (68%)
  between operations  14.2 us (11%)
  other arithmetic  10.7 us (8%)
  local copies, waits for them, and re-layouts  6.83 us (5%)
  starting transfers between devices  6.41 us (5%)
  matrix products  4.19 us (3%)
    reduce_scatter x1, waiting for transfers between devices, on_device(): lax.psum_scatter(lax.dot_general(arrived, row_grads, (((0,), (0,)), ((),...  39.4 us
    all_gather x1, waiting for transfers between devices, on_device(): grad_head = jnp.sum(lax.all_gather(sector_sums, 'frame'), axis=0)  31.9 us
    all_to_all x1, waiting for transfers between devices, on_device(): lax.all_to_all(packed, 'sector', split_axis=0, concat_axis=0, tiled=True)  20.7 us
    all_to_all x1, starting transfers between devices, on_device(): lax.all_to_all(packed, 'sector', split_axis=0, concat_axis=0, tiled=True)  6.33 us
    unnamed x14, local copies, waits for them, and re-layouts  4.64 us
    scatter-add x1, other arithmetic, on_device(): jax.ops.segment_sum(spread.reshape(blocks * per_block, unit_rows * head_w...  4.17 us
  transfers between devices with their start and end apart: 3, of which 3 were waited for; matrix products, arithmetic and copies ran while one was open for 0% of the time, Pallas kernels for 0%

profile of v1, /device:TPU:0, one launch (start us, length us, event | category | flops | bytes accessed | tf_op | source)
XLA Modules:
  0.0 134.3 jit_solution(17937041395037864326)
XLA Ops:
  7.2 0.0 copy-start
  7.2 1.3 reshape.112
  8.5 0.9 select_reduce_fusion
  9.4 0.7 multiply_add_fusion
  10.1 0.3 convolution_convert_fusion
  10.4 1.1 copy.10
  11.5 6.3 %all-to-all-start = ((bf16[8,2,16,1536]{3,2,1,0:T(8,128)(2,1)}), bf16[8,2,16,1536]{3,2,1,0:T(8,128)(2,1)S(1)}, u32[]{:S(2)}, u32[]{:S(2)}) async-start(bf16[8,2,16,1536]{3,2,1,0:T(8,128)(2,1)} %bitcast.20), calls=%async_computation | async-start | bytes 1572864 | tf_op jit(solution)/shard_map/all_to_all | solution.py:47
  17.8 0.0 reduce-scatter.2.cloned.1.call-start
  17.9 0.1 reshape.116
  18.0 0.1 reshape.131
  18.1 20.7 %all-to-all-done = bf16[8,2,16,1536]{3,2,1,0:T(8,128)(2,1)S(1)} async-done(((bf16[8,2,16,1536]{3,2,1,0:T(8,128)(2,1)}), bf16[8,2,16,1536]{3,2,1,0:T(8,128)(2,1)S(1)}, u32[]{:S(2)}, u32[]{:S(2)}) %all-to-all-start) | async-done | bytes 786464 | tf_op jit(solution)/shard_map/all_to_all | solution.py:47
  38.8 0.0 copy-done
  38.8 0.6 convolution_convert_fusion.1
  39.4 0.3 copy-done.2
  39.7 0.6 gather_fusion
  40.4 0.0 copy-start.1
  40.4 0.0 copy-done.4
  40.4 0.6 fusion.9
  41.0 0.6 copy-done.1
  41.6 0.4 fusion.1
  42.0 2.2 %fusion.7 = (bf16[1024,512]{1,0:T(8,128)(2,1)S(1)}, bf16[1024,512]{1,0:T(8,128)(2,1)}) fusion(bf16[1024,512]{1,0:T(8,128)(2,1)S(1)} %copy-done.1, f32[8,512,128,1]{1,2,3,0:T(8,128)S(1)} %get-tuple-element.11, f32[1024]{0:T(1024)S(1)} %get-tuple-element.8, f32[1024]{0:T(1024)S(1)} %get-tuple-element.4, f32[1024]{0:T(1024)S(1)} %get-tuple-element.5, ...), kind=kLoop, calls=%fused_computation.14 | loop fusion | flops 6815744 | bytes 5259264 | tf_op jit(solution)/shard_map/convert_element_type | solution.py:22
  44.2 0.4 convolution_bitcast_fusion
  44.6 2.5 %copy.11 = f32[8,8,16,512]{3,1,2,0:T(8,128)} copy(f32[8,8,16,512]{3,2,1,0:T(8,128)S(1)} %convolution_bitcast_fusion) | data formatting | bytes 4194304
  47.2 4.2 %scatter_custom_fusion = f32[16,8192]{1,0:T(8,128)S(1)} fusion(s32[64]{0:T(128)S(1)} %reshape.131, f32[64,8192]{1,0:T(8,128)} %bitcast.56, f32[]{:T(128)} %constant.8.clone.1), kind=kCustom, calls=%fused_computation.27 | custom fusion | flops 524288 | bytes 524800 | tf_op jit(solution)/shard_map/scatter-add | solution.py:64
  51.4 0.1 reshape.120
  51.5 2.3 %fusion.23 = f32[1536,512]{1,0:T(8,128)} fusion(bf16[256,1536]{1,0:T(8,128)(2,1)S(1)} %bitcast.54, bf16[256,512]{1,0:T(8,128)(2,1)S(1)} %reshape.120), kind=kOutput, calls=%fused_computation.47 | convolution fusion | flops 402653184 | bytes 4194304 | tf_op jit(solution)/shard_map/dot_general | solution.py:71
  53.8 0.0 reduce-scatter.2.cloned.1.call-update
  53.8 0.0 all-gather.3.cloned.1.call-start
  53.9 39.4 %reduce-scatter.2.cloned.1.call-done = f32[192,512]{1,0:T(8,128)} async-done(((f32[1536,512]{1,0:T(8,128)}), f32[192,512]{1,0:T(8,128)}) %reduce-scatter.2.cloned.1.call-update) | async-done | bytes 393232 | tf_op jit(solution)/shard_map/reduce_scatter | solution.py:70
  93.2 0.0 all-gather.3.cloned.1.call-update
  93.2 31.9 %all-gather.3.cloned.1.call-done = f32[768,512]{1,0:T(8,128)} async-done(((f32[192,512]{1,0:T(8,128)}), f32[768,512]{1,0:T(8,128)}) %all-gather.3.cloned.1.call-update) | async-done | bytes 1572880 | tf_op jit(solution)/shard_map/all_gather | solution.py:78
  125.2 2.3 %reduce_sum.49 = f32[192,512]{1,0:T(8,128)} reduce(f32[4,192,512]{2,1,0:T(8,128)} %bitcast.57, f32[]{:T(128)} %constant.8.clone.1), dimensions={0}, to_apply=%region_6.7 | reduce | flops 294912 | bytes 1966084 | tf_op jit(solution)/shard_map/reduce_sum | solution.py:78
  (11 shorter events, 0.1 us)
Async XLA Ops:
  7.2 31.7 %copy-start = (bf16[1536,512]{1,0:T(8,128)(2,1)S(1)}, bf16[1536,512]{1,0:T(8,128)(2,1)}, u32[]{:S(2)}) copy-start(bf16[1536,512]{1,0:T(8,128)(2,1)} %param.11) | copy-start | bytes 4718596
  10.1 7.8 %copy-start.5 = (s32[8,8]{1,0:T(8,128)S(1)}, s32[8,8]{1,0:T(8,128)}, u32[]{:S(2)}) copy-start(s32[8,8]{1,0:T(8,128)} %param.8) | copy-start | bytes 772
  11.5 27.3 %all-to-all-start = ((bf16[8,2,16,1536]{3,2,1,0:T(8,128)(2,1)}), bf16[8,2,16,1536]{3,2,1,0:T(8,128)(2,1)S(1)}, u32[]{:S(2)}, u32[]{:S(2)}) async-start(bf16[8,2,16,1536]{3,2,1,0:T(8,128)(2,1)} %bitcast.20), calls=%async_computation | async-start | bytes 1572864 | tf_op jit(solution)/shard_map/all_to_all | solution.py:47
  17.8 75.4 %reduce-scatter.2.cloned.1.call-start = ((), (), s32[]{:S(2)}) async-start(), calls=%async_computation.2 | async-start | bytes 3538944 | tf_op jit(solution)/shard_map/reduce_scatter | solution.py:70
  38.8 0.9 copy-start.2
  38.8 1.5 %copy-start.4 = (bf16[8,8,16,128]{3,2,1,0:T(8,128)(2,1)S(1)}, bf16[8,8,16,128]{3,2,1,0:T(8,128)(2,1)}, u32[]{:S(2)}) copy-start(bf16[8,8,16,128]{3,2,1,0:T(8,128)(2,1)} %param.9) | copy-start | bytes 786436
  40.4 1.2 copy-start.1
  44.6 6.9 %copy-start.3 = (bf16[8,2,16,1536]{3,2,1,0:T(8,128)(2,1)S(1)}, bf16[8,2,16,1536]{3,2,1,0:T(8,128)(2,1)}, u32[]{:S(2)}) copy-start(bf16[8,2,16,1536]{3,2,1,0:T(8,128)(2,1)} %copy-done.2) | copy-start | bytes 2359300
  53.8 71.3 %all-gather.3.cloned.1.call-start = ((), (), s32[]{:S(2)}) async-start(), calls=%async_computation.3 | async-start | bytes 1966080 | tf_op jit(solution)/shard_map/all_gather | solution.py:78
Sparse Core Ops, SparseCore 0:
  53.9 39.2 reduce-scatter.1
  95.1 30.0 all-gather.2
